TPU v7x, 32 devices: a whole 2x2x4 slice. The times are simulated.
32 devices in a mesh: heads: 2 (over core), tokens: 16 (over z, y, x).
Axes of the slice: x: 2, y: 2, z: 4, core: 2. Of those that a mesh axis runs over, the one named last changes fastest.
Arguments:
- queries: bfloat16 [2, 2048, 2048], P(None, 'tokens', 'heads'), may hold values from -8.5 to 8.5, as said below
- keys: bfloat16 [2, 2048, 2048], P(None, 'tokens', 'heads'), may hold values from -6 to 6
- values: bfloat16 [2, 2048, 2048], P(None, 'tokens', 'heads'), may hold values from -6 to 6
- rates: float32 [2, 8, 2048], P(None, 'heads', 'tokens'), may hold values from 0.05 to 1
- fast_init: bfloat16 [8, 3, 256, 256], P('heads'), may hold values from -0.375 to 0.375
- out_gain: float32 [2048], P('heads'), may hold values from 0.25 to 1.75
Outputs:
- mixed: bfloat16 [2, 2048, 2048], P(None, 'tokens', 'heads')
- final_weights: bfloat16 [8, 3, 256, 256], P('heads')
Inputs may be any that keep to these rules, and one draw needn't show every extreme that they name: queries are real-valued and of order one.
All inputs are finite; a program needn't handle non-finite values.
Results may differ from a plain program's by a relative error of at most 0.0095.
Values may be sent and summed in bfloat16 or wider, within the bound.
A program may use at most 64 MiB of HBM per device.

v0:
```python
import jax
import jax.numpy as jnp
from jax import lax
from jax.sharding import PartitionSpec as P

D = 2048
NS_STEPS = 2


coef_a = 3.4445
coef_b = -4.775
coef_c = 2.0315
step_size = 0.5


def newton(current):
    for step in range(NS_STEPS):
        gram = jnp.einsum(
            "hmij,hmkj->hmik", current, current, preferred_element_type=jnp.float32
        ).astype(jnp.bfloat16)
        square = jnp.einsum("hmij,hmjk->hmik", gram, gram, preferred_element_type=jnp.float32)
        mixer = (coef_b * gram.astype(jnp.float32) + coef_c * square).astype(jnp.bfloat16)
        product = jnp.einsum("hmij,hmjk->hmik", mixer, current, preferred_element_type=jnp.float32)
        current = (coef_a * current.astype(jnp.float32) + product).astype(jnp.bfloat16)
    return current


def apply_heads(query, weights):
    gate_q = jnp.einsum("nhd,hde->nhe", query, weights[:, 0], preferred_element_type=jnp.float32)
    up_q = jnp.einsum("nhd,hde->nhe", query, weights[:, 1], preferred_element_type=jnp.float32)
    hidden_q = (jax.nn.silu(gate_q) * up_q).astype(jnp.bfloat16)
    return jnp.einsum("nhd,hde->nhe", hidden_q, weights[:, 2], preferred_element_type=jnp.float32)


def local_grads(key_rows, value_rows, rate, weights):
    gate_k = jnp.einsum("nhd,hde->nhe", key_rows, weights[:, 0], preferred_element_type=jnp.float32)
    up_k = jnp.einsum("nhd,hde->nhe", key_rows, weights[:, 1], preferred_element_type=jnp.float32)
    sig = jax.nn.sigmoid(gate_k)
    hidden = (gate_k * sig * up_k).astype(jnp.bfloat16)
    scaled = (rate.T[:, :, None] * value_rows.astype(jnp.float32)).astype(jnp.bfloat16)
    back = jnp.einsum("nhe,hde->nhd", scaled, weights[:, 2], preferred_element_type=jnp.float32)
    grad_gate = (back * up_k * sig * (1.0 + gate_k * (1.0 - sig))).astype(jnp.bfloat16)
    grad_up = (back * gate_k * sig).astype(jnp.bfloat16)
    g_gate = jnp.einsum("nhd,nhe->hde", key_rows, grad_gate, preferred_element_type=jnp.float32)
    g_up = jnp.einsum("nhd,nhe->hde", key_rows, grad_up, preferred_element_type=jnp.float32)
    g_down = jnp.einsum("nhd,nhe->hde", hidden, scaled, preferred_element_type=jnp.float32)
    return jnp.stack([g_gate, g_up, g_down], axis=1)


def finish(joined, totals, out_gain):
    return (joined / jnp.sqrt(totals[:, None] / D + 1e-06) * out_gain[None, :]).astype(jnp.bfloat16)


def per_device(queries, keys, values, rates, fast_init, out_gain):
    heads_here = fast_init.shape[0]
    head_size = fast_init.shape[2]
    tok_rows = queries.shape[1]
    weights = fast_init
    outputs = []
    joined_all = []
    for block in range(queries.shape[0]):
        query = queries[block].reshape(tok_rows, heads_here, head_size)
        key_rows = keys[block].reshape(tok_rows, heads_here, head_size)
        value_rows = values[block].reshape(tok_rows, heads_here, head_size)
        joined = apply_heads(query, weights).reshape(tok_rows, heads_here * head_size)
        grads = local_grads(key_rows, value_rows, rates[block], weights)
        total = lax.psum(grads, "tokens")
        squares = jnp.sum(total * total, axis=(2, 3))
        start = (total / (jnp.sqrt(squares)[:, :, None, None] + 1e-07)).astype(jnp.bfloat16)
        update = newton(start)
        weights = (weights.astype(jnp.float32) + step_size * update.astype(jnp.float32)).astype(
            jnp.bfloat16
        )
        joined_all.append(joined)
    stacked = jnp.stack(joined_all, axis=0)
    totals = lax.psum(jnp.sum(stacked * stacked, axis=2), "heads")
    outputs = [
        finish(joined_all[index], totals[index], out_gain) for index in range(len(joined_all))
    ]
    return (jnp.stack(outputs, axis=0), weights)


def solution(mesh):
    in_specs = (
        P(None, "tokens", "heads"),
        P(None, "tokens", "heads"),
        P(None, "tokens", "heads"),
        P(None, "heads", "tokens"),
        P("heads", None, None, None),
        P("heads"),
    )
    out_specs = (P(None, "tokens", "heads"), P("heads", None, None, None))
    return jax.shard_map(
        per_device, mesh=mesh, in_specs=in_specs, out_specs=out_specs, check_vma=False
    )
```

profile of v0, /device:TPU:0, one launch (start us, length us, event | category | flops | bytes accessed | tf_op | source)
XLA Modules:
  0.0 344.5 jit_solution(11807205972683638040)
XLA Ops:
  7.2 1.9 fusion.54
  9.3 0.7 copy.39
  10.0 1.1 convolution_bitcast_fusion.11
  11.1 1.1 convolution_bitcast_fusion.12
  12.2 1.1 slice_convert_fusion
  13.3 2.1 reshape.169
  15.4 1.5 convolution_bitcast_fusion.13
  16.9 0.5 convolution_bitcast_fusion.3
  17.4 0.4 convolution_bitcast_fusion.5
  18.1 2.1 pad_maximum_fusion
  20.3 1.1 copy.132
  21.4 2.1 reshape.170
  23.5 146.6 %all-reduce.3.cloned.1.call-done = f32[4,3,256,256]{2,3,0,1:T(8,128)} async-done(((f32[4,3,256,256]{2,3,0,1:T(8,128)}), f32[4,3,256,256]{2,3,0,1:T(8,128)}) %all-reduce.3.cloned.1.call-update) | async-done | bytes 3145744 | tf_op jit(solution)/shard_map/psum | solution.py:67
  170.0 2.4 multiply_reduce_fusion.1
  172.4 0.4 copy-done.1
  172.9 0.4 divide_convert_fusion.1
  173.3 0.7 convolution_convert_fusion.3
  173.9 0.6 add_convert_fusion.9
  174.6 0.6 add_convert_fusion.8
  175.2 0.6 convolution_convert_fusion.2
  175.8 0.6 add_convert_fusion.7
  176.5 0.9 add_convert_fusion.5
  178.0 0.8 copy-done.5
  178.8 0.5 convolution_bitcast_fusion.8
  179.3 0.5 convolution_bitcast_fusion
  179.8 0.4 convolution_bitcast_fusion.2
  180.5 2.1 pad_maximum_fusion.1
  182.6 1.8 fusion.55
  184.3 0.8 copy.128
  185.2 1.1 copy.131
  186.3 2.1 convolution_bitcast_fusion.16
  188.4 2.4 convolution_bitcast_fusion.14
  190.8 1.3 copy.45
  192.2 1.3 convolution_bitcast_fusion.10
  193.5 0.5 fusion.16
  194.2 2.7 psum.22
  197.1 1.0 copy.82
  198.1 130.6 %all-reduce.5.cloned.1.call-done = f32[4,3,256,256]{2,3,0,1:T(8,128)} async-done(((f32[4,3,256,256]{2,3,0,1:T(8,128)}), f32[4,3,256,256]{2,3,0,1:T(8,128)}) %all-reduce.5.cloned.1.call-update) | async-done | bytes 3145744 | tf_op jit(solution)/shard_map/psum | solution.py:67
  328.8 2.4 multiply_reduce_fusion
  331.1 0.4 copy-done
  331.6 0.4 divide_convert_fusion
  332.0 0.7 convolution_convert_fusion.1
  332.7 0.6 add_convert_fusion.4
  333.3 0.6 add_convert_fusion.3
  334.0 0.6 convolution_convert_fusion
  334.6 0.6 add_convert_fusion.2
  335.2 0.9 add_convert_fusion
  336.1 1.6 copy.83
  (37 shorter events, 2.0 us)
Async XLA Ops:
  7.2 2.1 copy-start.2
  7.2 162.8 %all-reduce.3.cloned.1.call-start = ((), (), s32[]{:S(2)}) async-start(), calls=%async_computation | async-start | bytes 6291456 | tf_op jit(solution)/shard_map/psum | solution.py:67
  10.0 2.2 copy-start.11
  10.0 2.2 copy-start.7
  15.4 1.5 copy-start.6
  15.4 1.5 copy-start.8
  15.4 1.6 copy-start.9
  20.2 308.5 %all-reduce.5.cloned.1.call-start = ((), (), s32[]{:S(2)}) async-start(), calls=%async_computation.1 | async-start | bytes 6291456 | tf_op jit(solution)/shard_map/psum | solution.py:67
  170.0 2.8 copy-start.1
  177.4 1.9 copy-start.3
  177.4 1.4 copy-start.5
  190.8 2.7 copy-start.4
  193.5 3.3 copy-start.10
  328.8 2.8 copy-start
Sparse Core Ops, SparseCore 0:
  20.3 149.6 all-reduce.2
  182.7 146.0 all-reduce.4
where the time goes:
time: 345 us
  waiting for transfers between devices  277 us (80%)
  matrix products  21.5 us (6%)
  local copies, waits for them, and re-layouts  17.4 us (5%)
  between operations  14.4 us (4%)
  other arithmetic  11.3 us (3%)
    psum x2, waiting for transfers between devices, per_device(): total = lax.psum(grads, 'tokens')  277 us
    unnamed x31, local copies, waits for them, and re-layouts  8.28 us
  transfers between devices with their start and end apart: 2, of which 2 were waited for; matrix products, arithmetic and copies ran while one was open for 5% of the time, Pallas kernels for 0%

commit v1 on v0

--- a/solution.py
+++ b/solution.py
@@ -1,6 +1,10 @@
+import functools
+
 import jax
 import jax.numpy as jnp
 from jax import lax
+from jax.experimental import pallas as pl
+from jax.experimental.pallas import tpu as pltpu
 from jax.sharding import PartitionSpec as P
 
 D = 2048
@@ -80,6 +84,340 @@
     return (jnp.stack(outputs, axis=0), weights)
 
 
+F32 = jnp.float32
+BF16 = jnp.bfloat16
+MESH = pl.DeviceIdType.MESH
+DOWN_FIRST = (2, 0, 1)
+
+
+def mm(a, b):
+    return jnp.dot(a, b, preferred_element_type=F32)
+
+
+def mm_nt(a, b):
+    return lax.dot_general(a, b, (((1,), (1,)), ((), ())), preferred_element_type=F32)
+
+
+def mm_tn(a, b):
+    return lax.dot_general(a, b, (((0,), (0,)), ((), ())), preferred_element_type=F32)
+
+
+def orthogonalize(mats):
+    xs = []
+    for g in mats:
+        g = g.astype(F32)
+        square = jnp.sum(jnp.sum(g * g, axis=1, keepdims=True), axis=0, keepdims=True)
+        xs.append((g / (jnp.sqrt(square) + 1e-07)).astype(BF16))
+    for _ in range(NS_STEPS):
+        grams = [mm_nt(x, x).astype(BF16) for x in xs]
+        mixers = [(coef_b * a.astype(F32) + coef_c * mm(a, a)).astype(BF16) for a in grams]
+        xs = [(coef_a * x.astype(F32) + mm(b, x)).astype(BF16) for b, x in zip(mixers, xs)]
+    return xs
+
+
+def kernel(
+    sizes, q_hbm, k_hbm, v_hbm, r_hbm, w_hbm, gain_ref, mixed_hbm, wout_hbm,
+    q0, w0, rates, kv, q1, hid, dp, dg, du, gf, gb, rs, ag, w1, wfull, ysend, ybuf, y0, mix, sq, sqr,
+    loc_sem, a2a_s, a2a_r, rs_s, rs_r, ag_s, ag_r, col_s, col_r, fwd_s, fwd_r, y_s, y_r, sq_s, sq_r,
+):
+    cores, HL, G, rows, DH = sizes
+    width = HL * DH
+    part = DH // G
+    core = lax.axis_index("heads")
+    t = lax.axis_index("tokens")
+    z = t // G
+    p = t % G
+    sends = []
+
+    def remote(src, dst, send_sem, recv_sem, device, start=True):
+        copy = pltpu.make_async_remote_copy(
+            src_ref=src, dst_ref=dst, send_sem=send_sem, recv_sem=recv_sem,
+            device_id=device, device_id_type=MESH,
+        )
+        if start:
+            copy.start()
+            sends.append(copy)
+        return copy
+
+    def head_peer(j):
+        return (z + j) % HL
+
+    def plane_peer(j):
+        return (p + j) % G
+
+    def at(zz, pp):
+        return {"tokens": zz * G + pp}
+
+    def cols(h):
+        return pl.ds(pl.multiple_of(h * DH, DH), DH)
+
+    def part_rows(pp):
+        return pl.ds(pl.multiple_of(pp * part, part), part)
+
+    local_q = pltpu.make_async_copy(q_hbm.at[0], q0, loc_sem.at[0])
+    local_w = pltpu.make_async_copy(w_hbm, w0, loc_sem.at[1])
+    local_r = pltpu.make_async_copy(r_hbm, rates.at[z], loc_sem.at[2])
+    local_w.start()
+    local_q.start()
+    local_r.start()
+    pieces = [(k_hbm, 0), (v_hbm, 0), (k_hbm, 1), (v_hbm, 1), (q_hbm, 1)]
+
+    def landing(i):
+        return q1 if i == 4 else kv.at[i]
+
+    local_pieces = []
+    for i, (ref, block) in enumerate(pieces):
+        copy = pltpu.make_async_copy(ref.at[block, :, cols(z)], landing(i).at[z], loc_sem.at[3 + i])
+        copy.start()
+        local_pieces.append(copy)
+
+    barrier = pltpu.get_barrier_semaphore()
+    for j in range(1, HL):
+        pl.semaphore_signal(barrier, inc=1, device_id=at(head_peer(j), p), device_id_type=MESH)
+    for j in range(1, G):
+        pl.semaphore_signal(barrier, inc=1, device_id=at(z, plane_peer(j)), device_id_type=MESH)
+    for j in range(1, cores):
+        pl.semaphore_signal(barrier, inc=1, device_id={"heads": (core + j) % cores}, device_id_type=MESH)
+    pl.semaphore_wait(barrier, HL - 1 + G - 1 + cores - 1)
+
+    for j in range(1, HL):
+        remote(r_hbm, rates.at[z], a2a_s.at[5, j], a2a_r.at[5, z], at(head_peer(j), p))
+    for i, (ref, block) in enumerate(pieces):
+        for j in range(1, HL):
+            h = head_peer(j)
+            remote(ref.at[block, :, cols(h)], landing(i).at[z], a2a_s.at[i, j], a2a_r.at[i, z], at(h, p))
+
+    def arrived(buf, recv_sem, send_sem, device):
+        remote(buf, buf, send_sem, recv_sem, device, start=False).wait_recv()
+
+    def piece_arrived(i, j):
+        h = head_peer(j)
+        if j == 0:
+            local_pieces[i].wait()
+        else:
+            arrived(landing(i).at[h], a2a_r.at[i, h], a2a_s.at[i, j], at(h, p))
+
+    def share_squares(block, square):
+        sq[block] = jnp.broadcast_to(square, (rows, 128))
+        for j in range(1, cores):
+            remote(sq.at[block], sqr.at[block, core], sq_s.at[block, j], sq_r.at[block, core],
+                   {"heads": (core + j) % cores})
+
+    def finish_block(block, read):
+        total = sq[block]
+        for j in range(1, cores):
+            other = (core + j) % cores
+            arrived(sqr.at[block, other], sq_r.at[block, other], sq_s.at[block, j], {"heads": other})
+            total = total + sqr[block, other]
+        root = jnp.sqrt(total[:, :1] / (cores * width) + 1e-06)
+        for h in range(HL):
+            span = slice(h * DH, (h + 1) * DH)
+            mix[block, :, span] = (read(h) / root * gain_ref[:, span]).astype(BF16)
+        copy = pltpu.make_async_copy(mix.at[block], mixed_hbm.at[block], loc_sem.at[8 + block])
+        copy.start()
+        return copy
+
+    def fast_net(x, w_gate, w_up, w_down):
+        gate = mm(x, w_gate)
+        hidden = (jax.nn.silu(gate) * mm(x, w_up)).astype(BF16)
+        return mm(hidden, w_down)
+
+    local_w.wait()
+    local_q.wait()
+    square = jnp.zeros((rows, 1), F32)
+    for h in range(HL):
+        span = slice(h * DH, (h + 1) * DH)
+        y = fast_net(q0[:, span], w0[h, 0], w0[h, 1], w0[h, 2])
+        y0[:, span] = y
+        square = square + jnp.sum(y * y, axis=1, keepdims=True)
+    share_squares(0, square)
+
+    order = [0] + sorted(range(1, HL), key=lambda j: min(j, HL - j))
+
+    def gradients(block, weight):
+        for n, j in enumerate(order):
+            h = head_peer(j)
+            if block == 0:
+                if j == 0:
+                    local_r.wait()
+                else:
+                    arrived(rates.at[h], a2a_r.at[5, h], a2a_s.at[5, j], at(h, p))
+            piece_arrived(2 * block, j)
+            piece_arrived(2 * block + 1, j)
+            keys = kv[2 * block, h]
+            rate = jnp.broadcast_to(rates[h, block, pl.ds(z, 1), :], (rows, rows)).T[:, :1]
+            own = pl.ds(pl.multiple_of(h * rows, rows), rows)
+            gate = mm(keys, weight(0))
+            up = mm(keys, weight(1))
+            sig = jax.nn.sigmoid(gate)
+            hid[block, h] = (gate * sig * up).astype(BF16)
+            scaled = (rate * kv[2 * block + 1, h].astype(F32)).astype(BF16)
+            dp[block, h] = scaled
+            back = mm_nt(scaled, weight(2))
+            dg[block, h] = (back * up * sig * (1.0 + gate * (1.0 - sig))).astype(BF16)
+            du[block, h] = (back * gate * sig).astype(BF16)
+
+        keys = kv[2 * block].reshape(HL * rows, DH)
+        pairs = {
+            0: lambda: mm_tn(keys, dg[block].reshape(HL * rows, DH)),
+            1: lambda: mm_tn(keys, du[block].reshape(HL * rows, DH)),
+            2: lambda: mm_tn(hid[block].reshape(HL * rows, DH), dp[block].reshape(HL * rows, DH)),
+        }
+        for m in DOWN_FIRST:
+            grad = pairs[m]()
+            gf[block, m] = grad
+            gb[block, m] = grad.astype(BF16)
+            for j in range(1, G):
+                o = plane_peer(j)
+                remote(gb.at[block, m, part_rows(o)], rs.at[block, m, p], rs_s.at[block, m, j],
+                       rs_r.at[block, m, p], at(z, o))
+
+    def sum_parts(block):
+        for m in DOWN_FIRST:
+            total = gf[block, m, part_rows(p)]
+            for j in range(1, G):
+                o = plane_peer(j)
+                arrived(rs.at[block, m, o], rs_r.at[block, m, o], rs_s.at[block, m, j], at(z, o))
+                total = total + rs[block, m, o].astype(F32)
+            ag[block, m, part_rows(p)] = total.astype(BF16)
+            for j in range(1, G):
+                mine = ag.at[block, m, part_rows(p)]
+                remote(mine, mine, ag_s.at[block, m, j], ag_r.at[block, m, p], at(z, plane_peer(j)))
+
+    def summed(block, m):
+        for j in range(1, G):
+            o = plane_peer(j)
+            arrived(ag.at[block, m, part_rows(o)], ag_r.at[block, m, o], ag_s.at[block, m, j], at(z, o))
+        return ag[block, m]
+
+    gradients(0, lambda m: w0[z, m])
+    out0 = finish_block(0, lambda h: y0[:, h * DH:(h + 1) * DH])
+    sum_parts(0)
+    updates = orthogonalize([summed(0, m) for m in DOWN_FIRST])
+    for m, x in zip(DOWN_FIRST, updates):
+        w1[m] = (w0[z, m].astype(F32) + step_size * x.astype(F32)).astype(BF16)
+
+    gradients(1, lambda m: w1[m])
+    for j in order:
+        h = head_peer(j)
+        piece_arrived(4, j)
+        y = fast_net(q1[h], w1[0], w1[1], w1[2]).astype(BF16)
+        if j == 0:
+            ybuf[z] = y
+        else:
+            ysend[h] = y
+            remote(ysend.at[h], ybuf.at[z], y_s.at[j], y_r.at[z], at(h, p))
+    sum_parts(1)
+    for m in DOWN_FIRST:
+        (x,) = orthogonalize([summed(1, m)])
+        wfull[z, m] = (w1[m].astype(F32) + step_size * x.astype(F32)).astype(BF16)
+        for j in order[1:]:
+            mine = wfull.at[z, m, part_rows(p)]
+            remote(mine, mine, col_s.at[m, j], col_r.at[m, z], at(head_peer(j), p))
+    copies = [out0]
+    copy = pltpu.make_async_copy(wfull.at[z], wout_hbm.at[z], loc_sem.at[10])
+    copy.start()
+    copies.append(copy)
+
+    for j in order[1:]:
+        h = head_peer(j)
+        arrived(ybuf.at[h], y_r.at[h], y_s.at[j], at(h, p))
+    square = jnp.zeros((rows, 1), F32)
+    for h in range(HL):
+        y = ybuf[h].astype(F32)
+        square = square + jnp.sum(y * y, axis=1, keepdims=True)
+    share_squares(1, square)
+
+    for j in order[1:]:
+        h = head_peer(j)
+        for m in DOWN_FIRST:
+            mine = wfull.at[h, m, part_rows(p)]
+            arrived(mine, col_r.at[m, h], col_s.at[m, j], at(h, p))
+            for i in range(1, G):
+                remote(mine, mine, fwd_s.at[m, j, i], fwd_r.at[m, h, p], at(z, plane_peer(i)))
+
+    copies.append(finish_block(1, lambda h: ybuf[h].astype(F32)))
+    for j in order[1:]:
+        h = head_peer(j)
+        for m in DOWN_FIRST:
+            for i in range(1, G):
+                o = plane_peer(i)
+                arrived(wfull.at[h, m, part_rows(o)], fwd_r.at[m, h, o], fwd_s.at[m, j, i], at(z, o))
+        copy = pltpu.make_async_copy(wfull.at[h], wout_hbm.at[h], loc_sem.at[10 + j])
+        copy.start()
+        copies.append(copy)
+    for copy in sends:
+        copy.wait_send()
+    for copy in copies:
+        copy.wait()
+
+
+def one_kernel(cores, token_devices, queries, keys, values, rates, fast_init, out_gain):
+    blocks, rows, width = queries.shape
+    HL, _, DH, _ = fast_init.shape
+    G = token_devices // HL
+    dma = pltpu.SemaphoreType.DMA
+    tokens = (2, HL, rows, DH)
+    mats = (2, 3, DH, DH)
+    any_space = pl.BlockSpec(memory_space=pl.ANY)
+    return pl.pallas_call(
+        functools.partial(kernel, (cores, HL, G, rows, DH)),
+        out_shape=(
+            jax.ShapeDtypeStruct(queries.shape, BF16),
+            jax.ShapeDtypeStruct(fast_init.shape, BF16),
+        ),
+        in_specs=[any_space] * 5 + [pl.BlockSpec(memory_space=pltpu.VMEM)],
+        out_specs=(any_space, any_space),
+        scratch_shapes=[
+            pltpu.VMEM((rows, width), BF16),
+            pltpu.VMEM(fast_init.shape, BF16),
+            pltpu.VMEM((HL,) + rates.shape, F32),
+            pltpu.VMEM((4, HL, rows, DH), BF16),
+            pltpu.VMEM((HL, rows, DH), BF16),
+            pltpu.VMEM(tokens, BF16),
+            pltpu.VMEM(tokens, BF16),
+            pltpu.VMEM(tokens, BF16),
+            pltpu.VMEM(tokens, BF16),
+            pltpu.VMEM(mats, F32),
+            pltpu.VMEM(mats, BF16),
+            pltpu.VMEM((2, 3, G, DH // G, DH), BF16),
+            pltpu.VMEM(mats, BF16),
+            pltpu.VMEM((3, DH, DH), BF16),
+            pltpu.VMEM(fast_init.shape, BF16),
+            pltpu.VMEM((HL, rows, DH), BF16),
+            pltpu.VMEM((HL, rows, DH), BF16),
+            pltpu.VMEM((rows, width), F32),
+            pltpu.VMEM(queries.shape, BF16),
+            pltpu.VMEM((2, rows, 128), F32),
+            pltpu.VMEM((2, cores, rows, 128), F32),
+            dma((10 + HL,)),
+            dma((6, HL)), dma((6, HL)),
+            dma((2, 3, G)), dma((2, 3, G)),
+            dma((2, 3, G)), dma((2, 3, G)),
+            dma((3, HL)), dma((3, HL)),
+            dma((3, HL, G)), dma((3, HL, G)),
+            dma((HL,)), dma((HL,)),
+            dma((2, cores)), dma((2, cores)),
+        ],
+        compiler_params=pltpu.CompilerParams(collective_id=0, has_side_effects=True),
+    )(queries, keys, values, rates, fast_init, out_gain.reshape(1, width))
+
+
+def fits(cores, token_devices, queries, fast_init):
+    blocks, rows, width = queries.shape
+    HL, _, DH, _ = fast_init.shape
+    if blocks != 2 or HL < 2 or token_devices % HL:
+        return False
+    G = token_devices // HL
+    return G > 1 and rows == 128 and DH % (16 * G) == 0 and cores > 1
+
+
+def per_device_best(cores, token_devices, queries, keys, values, rates, fast_init, out_gain):
+    if fits(cores, token_devices, queries, fast_init):
+        return one_kernel(cores, token_devices, queries, keys, values, rates, fast_init, out_gain)
+    return per_device(queries, keys, values, rates, fast_init, out_gain)
+
+
 def solution(mesh):
     in_specs = (
         P(None, "tokens", "heads"),
@@ -91,5 +429,5 @@
     )
     out_specs = (P(None, "tokens", "heads"), P("heads", None, None, None))
     return jax.shard_map(
-        per_device, mesh=mesh, in_specs=in_specs, out_specs=out_specs, check_vma=False
+        functools.partial(per_device_best, mesh.shape["heads"], mesh.shape["tokens"]), mesh=mesh, in_specs=in_specs, out_specs=out_specs, check_vma=False
     )

time: 345 us -> 71.4 us (0.21)
  waiting for transfers between devices: 277 us -> 0 us
  Pallas kernels: 0 us -> 66 us
  matrix products: 21.5 us -> 0 us
  between operations: 14.4 us -> 0.64 us
  local copies, waits for them, and re-layouts: 17.4 us -> 4.52 us
  other arithmetic: 11.3 us -> 0 us
    psum x2 -> x0, waiting for transfers between devices: 277 us -> none  [per_device(): total = lax.psum(grads, 'tokens')]
    pallas_call x0 -> x1, Pallas kernels: none -> 66 us  [one_kernel(): pl.pallas_call(functools.partial(kernel, (cores, HL, G, rows, DH)), out_s...]
    dot_general x28 -> x0, matrix products: 21.5 us -> none  [the longest x2 3.38 us: apply_heads(): jnp.einsum('nhd,hde->nhe', query, weights[:, 0], preferred_element_type=j...]
    reduce_sum x3 -> x0, other arithmetic: 4.91 us -> none  [the longest x2 4.76 us: per_device(): squares = jnp.sum(total * total, axis=(2, 3))]
    another operation x3 -> x0, other arithmetic: 4.2 us -> none  [the longest x2 4.14 us: local_grads(): return jnp.stack([g_gate, g_up, g_down], axis=1)]
    convert_element_type x2 -> x0, local copies, waits for them, and re-layouts: 4.15 us -> none  [local_grads(): value_rows.astype(jnp.float32)]
    unnamed x31 -> x2, local copies, waits for them, and re-layouts: 8.28 us -> 4.52 us
    slice x2 -> x0, local copies, waits for them, and re-layouts: 3.64 us -> none  [the longest x1 1.87 us: per_device(): key_rows = keys[block].reshape(tok_rows, heads_here, head_size)]
  transfers between devices with their start and end apart: 2 -> 0, of which waited for: 2 -> 0; matrix products, arithmetic and copies ran while one was open for 5% -> 0% of each run, Pallas kernels for 0% -> 0%
where the time goes in v1:
time: 71.4 us; the launch traced here: 71.2 us
  Pallas kernels  66 us (92%)
  local copies, waits for them, and re-layouts  4.52 us (6%)
    pallas_call x1, Pallas kernels, one_kernel(): pl.pallas_call(functools.partial(kernel, (cores, HL, G, rows, DH)), out_s...  66 us
    unnamed x2, local copies, waits for them, and re-layouts  4.52 us

profile of v1, /device:TPU:0, one launch (start us, length us, event | category | flops | bytes accessed | tf_op | source)
XLA Modules:
  0.0 71.2 jit_solution(5815373666731115148)
XLA Ops:
  0.6 66.0 %shard_map.77 = (bf16[2,128,1024]{2,1,0:T(8,128)(2,1)}, bf16[4,3,256,256]{3,2,1,0:T(8,128)(2,1)}) custom-call(bf16[2,128,1024]{2,1,0:T(8,128)(2,1)} %q_hbm.1, bf16[2,128,1024]{2,1,0:T(8,128)(2,1)} %k_hbm.1, bf16[2,128,1024]{2,1,0:T(8,128)(2,1)} %v_hbm.1, f32[2,4,128]{2,1,0:T(4,128)} %r_hbm.1, bf16[4,3,256,256]{3,2,1,0:T(8,128)(2,1)} %w_hbm.1, f32[1,1024]{1,0:T(1,128)} %bitcast.1), custom_call_target="tpu_custom_call" | custom-call | tf_op jit(solution)/shard_map/pallas_call | solution.py:363
  66.7 1.9 %copy.10 = bf16[2,128,1024]{2,1,0:T(8,128)(2,1)} copy(bf16[2,128,1024]{2,1,0:T(8,128)(2,1)} %get-tuple-element.4) | data formatting | bytes 1048576
  68.6 2.7 %copy.11 = bf16[4,3,256,256]{3,2,1,0:T(8,128)(2,1)} copy(bf16[4,3,256,256]{3,2,1,0:T(8,128)(2,1)} %get-tuple-element.5) | data formatting | bytes 3145728

commit v2 on v1

--- a/solution.py
+++ b/solution.py
@@ -116,9 +116,9 @@
 
 
 def kernel(
-    sizes, q_hbm, k_hbm, v_hbm, r_hbm, w_hbm, gain_ref, mixed_hbm, wout_hbm,
-    q0, w0, rates, kv, q1, hid, dp, dg, du, gf, gb, rs, ag, w1, wfull, ysend, ybuf, y0, mix, sq, sqr,
-    loc_sem, a2a_s, a2a_r, rs_s, rs_r, ag_s, ag_r, col_s, col_r, fwd_s, fwd_r, y_s, y_r, sq_s, sq_r,
+    sizes, q_hbm, k_hbm, v_hbm, r_hbm, w_hbm, gain_hbm, mixed, wout,
+    q0, w0, rates, gain, kv, q1, hid, dp, dg, du, gf, gb, rs, ag, w1, ysend, ybuf, y0, sq, sqr,
+    loc_sem, a2a_s, kv_r, one_r, rs_s, rs_r, ag_s, ag_r, col_s, col_r, fwd_s, fwd_r, y_s, sq_s, sq_r,
 ):
     cores, HL, G, rows, DH = sizes
     width = HL * DH
@@ -127,26 +127,36 @@
     t = lax.axis_index("tokens")
     z = t // G
     p = t % G
-    sends = []
-
-    def remote(src, dst, send_sem, recv_sem, device, start=True):
-        copy = pltpu.make_async_remote_copy(
+    xn = p + 1 - 2 * (p % 2)
+    yn = (p + 2) % G
+    across = (xn + 2) % G
+
+    def remote(src, dst, send_sem, recv_sem, device):
+        return pltpu.make_async_remote_copy(
             src_ref=src, dst_ref=dst, send_sem=send_sem, recv_sem=recv_sem,
             device_id=device, device_id_type=MESH,
         )
-        if start:
-            copy.start()
-            sends.append(copy)
-        return copy
+
+    def send(src, dst, send_sem, recv_sem, device):
+        remote(src, dst, send_sem, recv_sem, device).start()
 
     def head_peer(j):
         return (z + j) % HL
 
+    def head_source(j):
+        return (z + HL - j) % HL
+
     def plane_peer(j):
         return (p + j) % G
 
     def at(zz, pp):
         return {"tokens": zz * G + pp}
+
+    def arrived(ref, recv_sem):
+        remote(ref, ref, loc_sem.at[0], recv_sem, at(z, xn)).wait_recv()
+
+    def drained(ref, send_sem):
+        remote(ref, ref, send_sem, loc_sem.at[0], at(z, xn)).wait_send()
 
     def cols(h):
         return pl.ds(pl.multiple_of(h * DH, DH), DH)
@@ -157,9 +167,11 @@
     local_q = pltpu.make_async_copy(q_hbm.at[0], q0, loc_sem.at[0])
     local_w = pltpu.make_async_copy(w_hbm, w0, loc_sem.at[1])
     local_r = pltpu.make_async_copy(r_hbm, rates.at[z], loc_sem.at[2])
+    local_gain = pltpu.make_async_copy(gain_hbm, gain, loc_sem.at[3])
     local_w.start()
     local_q.start()
     local_r.start()
+    local_gain.start()
     pieces = [(k_hbm, 0), (v_hbm, 0), (k_hbm, 1), (v_hbm, 1), (q_hbm, 1)]
 
     def landing(i):
@@ -167,7 +179,7 @@
 
     local_pieces = []
     for i, (ref, block) in enumerate(pieces):
-        copy = pltpu.make_async_copy(ref.at[block, :, cols(z)], landing(i).at[z], loc_sem.at[3 + i])
+        copy = pltpu.make_async_copy(ref.at[block, :, cols(z)], landing(i).at[z], loc_sem.at[4 + i])
         copy.start()
         local_pieces.append(copy)
 
@@ -181,46 +193,43 @@
     pl.semaphore_wait(barrier, HL - 1 + G - 1 + cores - 1)
 
     for j in range(1, HL):
-        remote(r_hbm, rates.at[z], a2a_s.at[5, j], a2a_r.at[5, z], at(head_peer(j), p))
+        send(r_hbm, rates.at[z], a2a_s.at[5], one_r.at[0], at(head_peer(j), p))
     for i, (ref, block) in enumerate(pieces):
         for j in range(1, HL):
             h = head_peer(j)
-            remote(ref.at[block, :, cols(h)], landing(i).at[z], a2a_s.at[i, j], a2a_r.at[i, z], at(h, p))
-
-    def arrived(buf, recv_sem, send_sem, device):
-        remote(buf, buf, send_sem, recv_sem, device, start=False).wait_recv()
-
-    def piece_arrived(i, j):
-        h = head_peer(j)
-        if j == 0:
-            local_pieces[i].wait()
-        else:
-            arrived(landing(i).at[h], a2a_r.at[i, h], a2a_s.at[i, j], at(h, p))
+            recv = one_r.at[1] if i == 4 else kv_r.at[block, j - 1]
+            send(ref.at[block, :, cols(h)], landing(i).at[z], a2a_s.at[i], recv, at(h, p))
 
     def share_squares(block, square):
         sq[block] = jnp.broadcast_to(square, (rows, 128))
         for j in range(1, cores):
-            remote(sq.at[block], sqr.at[block, core], sq_s.at[block, j], sq_r.at[block, core],
-                   {"heads": (core + j) % cores})
+            send(sq.at[block], sqr.at[block, j - 1], sq_s.at[block], sq_r.at[block],
+                 {"heads": (core + j) % cores})
 
     def finish_block(block, read):
         total = sq[block]
+        arrived(sqr.at[block], sq_r.at[block])
         for j in range(1, cores):
-            other = (core + j) % cores
-            arrived(sqr.at[block, other], sq_r.at[block, other], sq_s.at[block, j], {"heads": other})
-            total = total + sqr[block, other]
+            total = total + sqr[block, j - 1]
         root = jnp.sqrt(total[:, :1] / (cores * width) + 1e-06)
         for h in range(HL):
             span = slice(h * DH, (h + 1) * DH)
-            mix[block, :, span] = (read(h) / root * gain_ref[:, span]).astype(BF16)
-        copy = pltpu.make_async_copy(mix.at[block], mixed_hbm.at[block], loc_sem.at[8 + block])
-        copy.start()
-        return copy
+            mixed[block, :, span] = (read(h) / root * gain[:, span]).astype(BF16)
 
     def fast_net(x, w_gate, w_up, w_down):
         gate = mm(x, w_gate)
         hidden = (jax.nn.silu(gate) * mm(x, w_up)).astype(BF16)
         return mm(hidden, w_down)
+
+    def share(view, send_sem, recv_x, recv_y, recv_r):
+        mine = view(part_rows(p))
+        send(mine, mine, send_sem, recv_x, at(z, xn))
+        send(mine, mine, send_sem, recv_y, at(z, yn))
+        send(mine, mine, send_sem, recv_r, at(z, across))
+
+    def shared(view, recv_x, recv_y):
+        arrived(view(part_rows(xn)), recv_x)
+        arrived(view(part_rows(yn)), recv_y)
 
     local_w.wait()
     local_q.wait()
@@ -235,18 +244,18 @@
     order = [0] + sorted(range(1, HL), key=lambda j: min(j, HL - j))
 
     def gradients(block, weight):
-        for n, j in enumerate(order):
-            h = head_peer(j)
-            if block == 0:
-                if j == 0:
+        for j in order:
+            h = head_source(j)
+            if j == 0:
+                local_pieces[2 * block].wait()
+                local_pieces[2 * block + 1].wait()
+                if block == 0:
                     local_r.wait()
-                else:
-                    arrived(rates.at[h], a2a_r.at[5, h], a2a_s.at[5, j], at(h, p))
-            piece_arrived(2 * block, j)
-            piece_arrived(2 * block + 1, j)
+                    arrived(rates.at[pl.ds(0, HL - 1)], one_r.at[0])
+            else:
+                arrived(kv.at[pl.ds(2 * block, 2), h], kv_r.at[block, j - 1])
             keys = kv[2 * block, h]
             rate = jnp.broadcast_to(rates[h, block, pl.ds(z, 1), :], (rows, rows)).T[:, :1]
-            own = pl.ds(pl.multiple_of(h * rows, rows), rows)
             gate = mm(keys, weight(0))
             up = mm(keys, weight(1))
             sig = jax.nn.sigmoid(gate)
@@ -256,7 +265,6 @@
             back = mm_nt(scaled, weight(2))
             dg[block, h] = (back * up * sig * (1.0 + gate * (1.0 - sig))).astype(BF16)
             du[block, h] = (back * gate * sig).astype(BF16)
-
         keys = kv[2 * block].reshape(HL * rows, DH)
         pairs = {
             0: lambda: mm_tn(keys, dg[block].reshape(HL * rows, DH)),
@@ -269,109 +277,104 @@
             gb[block, m] = grad.astype(BF16)
             for j in range(1, G):
                 o = plane_peer(j)
-                remote(gb.at[block, m, part_rows(o)], rs.at[block, m, p], rs_s.at[block, m, j],
-                       rs_r.at[block, m, p], at(z, o))
+                send(gb.at[block, m, part_rows(o)], rs.at[block, m, j - 1], rs_s.at[block],
+                     rs_r.at[block, m], at(z, o))
+
+    def ag_view(block, m):
+        return lambda span: ag.at[block, m, span]
 
     def sum_parts(block):
         for m in DOWN_FIRST:
             total = gf[block, m, part_rows(p)]
+            arrived(rs.at[block, m], rs_r.at[block, m])
             for j in range(1, G):
-                o = plane_peer(j)
-                arrived(rs.at[block, m, o], rs_r.at[block, m, o], rs_s.at[block, m, j], at(z, o))
-                total = total + rs[block, m, o].astype(F32)
+                total = total + rs[block, m, j - 1].astype(F32)
             ag[block, m, part_rows(p)] = total.astype(BF16)
-            for j in range(1, G):
-                mine = ag.at[block, m, part_rows(p)]
-                remote(mine, mine, ag_s.at[block, m, j], ag_r.at[block, m, p], at(z, plane_peer(j)))
+            share(ag_view(block, m), ag_s.at[block], ag_r.at[block, m, 0], ag_r.at[block, m, 1], ag_r.at[block, m, 2])
+        for m in DOWN_FIRST:
+            shared(ag_view(block, m), ag_r.at[block, m, 0], ag_r.at[block, m, 1])
 
     def summed(block, m):
-        for j in range(1, G):
-            o = plane_peer(j)
-            arrived(ag.at[block, m, part_rows(o)], ag_r.at[block, m, o], ag_s.at[block, m, j], at(z, o))
+        arrived(ag.at[block, m, part_rows(across)], ag_r.at[block, m, 2])
         return ag[block, m]
 
     gradients(0, lambda m: w0[z, m])
-    out0 = finish_block(0, lambda h: y0[:, h * DH:(h + 1) * DH])
+    local_gain.wait()
+    finish_block(0, lambda h: y0[:, h * DH:(h + 1) * DH])
     sum_parts(0)
     updates = orthogonalize([summed(0, m) for m in DOWN_FIRST])
     for m, x in zip(DOWN_FIRST, updates):
         w1[m] = (w0[z, m].astype(F32) + step_size * x.astype(F32)).astype(BF16)
 
     gradients(1, lambda m: w1[m])
+    local_pieces[4].wait()
+    arrived(q1.at[pl.ds(0, HL - 1)], one_r.at[1])
     for j in order:
         h = head_peer(j)
-        piece_arrived(4, j)
         y = fast_net(q1[h], w1[0], w1[1], w1[2]).astype(BF16)
         if j == 0:
             ybuf[z] = y
         else:
             ysend[h] = y
-            remote(ysend.at[h], ybuf.at[z], y_s.at[j], y_r.at[z], at(h, p))
+            send(ysend.at[h], ybuf.at[z], y_s.at[0], one_r.at[2], at(h, p))
     sum_parts(1)
     for m in DOWN_FIRST:
         (x,) = orthogonalize([summed(1, m)])
-        wfull[z, m] = (w1[m].astype(F32) + step_size * x.astype(F32)).astype(BF16)
+        wout[z, m] = (w1[m].astype(F32) + step_size * x.astype(F32)).astype(BF16)
         for j in order[1:]:
-            mine = wfull.at[z, m, part_rows(p)]
-            remote(mine, mine, col_s.at[m, j], col_r.at[m, z], at(head_peer(j), p))
-    copies = [out0]
-    copy = pltpu.make_async_copy(wfull.at[z], wout_hbm.at[z], loc_sem.at[10])
-    copy.start()
-    copies.append(copy)
-
-    for j in order[1:]:
-        h = head_peer(j)
-        arrived(ybuf.at[h], y_r.at[h], y_s.at[j], at(h, p))
+            mine = wout.at[z, m, part_rows(p)]
+            send(mine, mine, col_s.at[0], col_r.at[m, j - 1], at(head_peer(j), p))
+
+    arrived(ybuf.at[pl.ds(0, HL - 1)], one_r.at[2])
     square = jnp.zeros((rows, 1), F32)
     for h in range(HL):
         y = ybuf[h].astype(F32)
         square = square + jnp.sum(y * y, axis=1, keepdims=True)
     share_squares(1, square)
 
-    for j in order[1:]:
-        h = head_peer(j)
-        for m in DOWN_FIRST:
-            mine = wfull.at[h, m, part_rows(p)]
-            arrived(mine, col_r.at[m, h], col_s.at[m, j], at(h, p))
-            for i in range(1, G):
-                remote(mine, mine, fwd_s.at[m, j, i], fwd_r.at[m, h, p], at(z, plane_peer(i)))
-
-    copies.append(finish_block(1, lambda h: ybuf[h].astype(F32)))
-    for j in order[1:]:
-        h = head_peer(j)
-        for m in DOWN_FIRST:
-            for i in range(1, G):
-                o = plane_peer(i)
-                arrived(wfull.at[h, m, part_rows(o)], fwd_r.at[m, h, o], fwd_s.at[m, j, i], at(z, o))
-        copy = pltpu.make_async_copy(wfull.at[h], wout_hbm.at[h], loc_sem.at[10 + j])
-        copy.start()
-        copies.append(copy)
-    for copy in sends:
-        copy.wait_send()
-    for copy in copies:
-        copy.wait()
+    def wout_view(m, j):
+        return lambda span: wout.at[head_source(j), m, span]
+
+    items = [(m, j) for m in DOWN_FIRST for j in order[1:]]
+    for m, j in items:
+        arrived(wout_view(m, j)(part_rows(p)), col_r.at[m, j - 1])
+        share(wout_view(m, j), fwd_s.at[0], fwd_r.at[0, m, j - 1], fwd_r.at[1, m, j - 1], one_r.at[3])
+    for m, j in items:
+        shared(wout_view(m, j), fwd_r.at[0, m, j - 1], fwd_r.at[1, m, j - 1])
+    finish_block(1, lambda h: ybuf[h].astype(F32))
+    arrived(wout.at[pl.ds(0, HL - 1), :, pl.ds(0, part)], one_r.at[3])
+
+    for i in range(5):
+        drained(q1.at[pl.ds(0, HL - 1)], a2a_s.at[i])
+    drained(rates.at[pl.ds(0, HL - 1)], a2a_s.at[5])
+    for block in range(2):
+        drained(rs.at[block], rs_s.at[block])
+        drained(rs.at[block], ag_s.at[block])
+        drained(sqr.at[block], sq_s.at[block])
+    drained(wout.at[pl.ds(0, HL - 1), :, pl.ds(0, part)], col_s.at[0])
+    drained(wout.at[pl.ds(0, HL - 1), :, pl.ds(0, 3 * part)], fwd_s.at[0])
+    drained(ysend.at[pl.ds(0, HL - 1)], y_s.at[0])
 
 
 def one_kernel(cores, token_devices, queries, keys, values, rates, fast_init, out_gain):
     blocks, rows, width = queries.shape
     HL, _, DH, _ = fast_init.shape
     G = token_devices // HL
-    dma = pltpu.SemaphoreType.DMA
+    dma = lambda *shape: pltpu.SemaphoreType.DMA(shape)
     tokens = (2, HL, rows, DH)
     mats = (2, 3, DH, DH)
     any_space = pl.BlockSpec(memory_space=pl.ANY)
+    in_vmem = pl.BlockSpec(memory_space=pltpu.VMEM)
     return pl.pallas_call(
         functools.partial(kernel, (cores, HL, G, rows, DH)),
-        out_shape=(
-            jax.ShapeDtypeStruct(queries.shape, BF16),
-            jax.ShapeDtypeStruct(fast_init.shape, BF16),
-        ),
-        in_specs=[any_space] * 5 + [pl.BlockSpec(memory_space=pltpu.VMEM)],
-        out_specs=(any_space, any_space),
+        out_shape=(pltpu.VMEM(queries.shape, BF16), pltpu.VMEM(fast_init.shape, BF16)),
+        in_specs=[any_space] * 6,
+        out_specs=(in_vmem, in_vmem),
         scratch_shapes=[
             pltpu.VMEM((rows, width), BF16),
             pltpu.VMEM(fast_init.shape, BF16),
             pltpu.VMEM((HL,) + rates.shape, F32),
+            pltpu.VMEM((1, width), F32),
             pltpu.VMEM((4, HL, rows, DH), BF16),
             pltpu.VMEM((HL, rows, DH), BF16),
             pltpu.VMEM(tokens, BF16),
@@ -380,24 +383,21 @@
             pltpu.VMEM(tokens, BF16),
             pltpu.VMEM(mats, F32),
             pltpu.VMEM(mats, BF16),
-            pltpu.VMEM((2, 3, G, DH // G, DH), BF16),
+            pltpu.VMEM((2, 3, G - 1, DH // G, DH), BF16),
             pltpu.VMEM(mats, BF16),
             pltpu.VMEM((3, DH, DH), BF16),
-            pltpu.VMEM(fast_init.shape, BF16),
             pltpu.VMEM((HL, rows, DH), BF16),
             pltpu.VMEM((HL, rows, DH), BF16),
             pltpu.VMEM((rows, width), F32),
-            pltpu.VMEM(queries.shape, BF16),
             pltpu.VMEM((2, rows, 128), F32),
-            pltpu.VMEM((2, cores, rows, 128), F32),
-            dma((10 + HL,)),
-            dma((6, HL)), dma((6, HL)),
-            dma((2, 3, G)), dma((2, 3, G)),
-            dma((2, 3, G)), dma((2, 3, G)),
-            dma((3, HL)), dma((3, HL)),
-            dma((3, HL, G)), dma((3, HL, G)),
-            dma((HL,)), dma((HL,)),
-            dma((2, cores)), dma((2, cores)),
+            pltpu.VMEM((2, cores - 1, rows, 128), F32),
+            dma(9),
+            dma(6), dma(2, HL - 1), dma(4),
+            dma(2), dma(2, 3),
+            dma(2), dma(2, 3, 3),
+            dma(1), dma(3, HL - 1),
+            dma(1), dma(2, 3, HL - 1),
+            dma(1), dma(2), dma(2),
         ],
         compiler_params=pltpu.CompilerParams(collective_id=0, has_side_effects=True),
     )(queries, keys, values, rates, fast_init, out_gain.reshape(1, width))
@@ -406,10 +406,10 @@
 def fits(cores, token_devices, queries, fast_init):
     blocks, rows, width = queries.shape
     HL, _, DH, _ = fast_init.shape
-    if blocks != 2 or HL < 2 or token_devices % HL:
-        return False
-    G = token_devices // HL
-    return G > 1 and rows == 128 and DH % (16 * G) == 0 and cores > 1
+    return (
+        blocks == 2 and HL > 1 and cores > 1 and token_devices == 4 * HL
+        and rows == 128 and DH % 128 == 0
+    )
 
 
 def per_device_best(cores, token_devices, queries, keys, values, rates, fast_init, out_gain):

time: 71.4 us -> 65.8 us (0.922)
  Pallas kernels: 66 us -> 63.1 us
  local copies, waits for them, and re-layouts: 4.52 us -> 1.94 us
    pallas_call x1, Pallas kernels: 66 us -> 63.1 us  [one_kernel(): pl.pallas_call(functools.partial(kernel, (cores, HL, G, rows, DH)), out_s...]
    unnamed x2, local copies, waits for them, and re-layouts: 4.52 us -> 1.94 us
where the time goes in v2:
time: 65.8 us; the launch traced here: 65.7 us
  Pallas kernels  63.1 us (96%)
  local copies, waits for them, and re-layouts  1.94 us (3%)
    pallas_call x1, Pallas kernels, one_kernel(): pl.pallas_call(functools.partial(kernel, (cores, HL, G, rows, DH)), out_s...  63.1 us
    unnamed x2, local copies, waits for them, and re-layouts  1.94 us

profile of v2, /device:TPU:0, one launch (start us, length us, event | category | flops | bytes accessed | tf_op | source)
XLA Modules:
  0.0 65.7 jit_solution(4339022786732608712)
XLA Ops:
  0.6 63.1 %shard_map.77 = (bf16[2,128,1024]{2,1,0:T(8,128)(2,1)S(1)}, bf16[4,3,256,256]{3,2,1,0:T(8,128)(2,1)S(1)}) custom-call(bf16[2,128,1024]{2,1,0:T(8,128)(2,1)} %q_hbm.1, bf16[2,128,1024]{2,1,0:T(8,128)(2,1)} %k_hbm.1, bf16[2,128,1024]{2,1,0:T(8,128)(2,1)} %v_hbm.1, f32[2,4,128]{2,1,0:T(4,128)} %r_hbm.1, bf16[4,3,256,256]{3,2,1,0:T(8,128)(2,1)} %w_hbm.1, ...), custom_call_target="tpu_custom_call" | custom-call | tf_op jit(solution)/shard_map/pallas_call | solution.py:368
  63.7 0.8 %copy.10 = bf16[2,128,1024]{2,1,0:T(8,128)(2,1)} copy(bf16[2,128,1024]{2,1,0:T(8,128)(2,1)S(1)} %get-tuple-element.2) | data formatting | bytes 1048576
  64.5 1.1 %copy.11 = bf16[4,3,256,256]{3,2,1,0:T(8,128)(2,1)} copy(bf16[4,3,256,256]{3,2,1,0:T(8,128)(2,1)S(1)} %get-tuple-element.3) | data formatting | bytes 3145728

commit v3 on v2

--- a/solution.py
+++ b/solution.py
@@ -123,6 +123,7 @@
     cores, HL, G, rows, DH = sizes
     width = HL * DH
     part = DH // G
+    half = part // 2
     core = lax.axis_index("heads")
     t = lax.axis_index("tokens")
     z = t // G
@@ -163,6 +164,9 @@
 
     def part_rows(pp):
         return pl.ds(pl.multiple_of(pp * part, part), part)
+
+    def half_rows(pp, which):
+        return pl.ds(pl.multiple_of(pp * part + which * half, half), half)
 
     local_q = pltpu.make_async_copy(q_hbm.at[0], q0, loc_sem.at[0])
     local_w = pltpu.make_async_copy(w_hbm, w0, loc_sem.at[1])
@@ -230,6 +234,14 @@
     def shared(view, recv_x, recv_y):
         arrived(view(part_rows(xn)), recv_x)
         arrived(view(part_rows(yn)), recv_y)
+
+    def pass_on(view, send_sem, recv_x, recv_y, recv_relay):
+        arrived(view(part_rows(xn)), recv_x)
+        first = view(half_rows(xn, 0))
+        send(first, first, send_sem, recv_relay, at(z, yn))
+        arrived(view(part_rows(yn)), recv_y)
+        second = view(half_rows(yn, 1))
+        send(second, second, send_sem, recv_relay, at(z, xn))
 
     local_w.wait()
     local_q.wait()
@@ -336,11 +348,25 @@
         return lambda span: wout.at[head_source(j), m, span]
 
     items = [(m, j) for m in DOWN_FIRST for j in order[1:]]
-    for m, j in items:
-        arrived(wout_view(m, j)(part_rows(p)), col_r.at[m, j - 1])
-        share(wout_view(m, j), fwd_s.at[0], fwd_r.at[0, m, j - 1], fwd_r.at[1, m, j - 1], one_r.at[3])
-    for m, j in items:
-        shared(wout_view(m, j), fwd_r.at[0, m, j - 1], fwd_r.at[1, m, j - 1])
+    passed = len(items) - 3
+    for n in range(len(items) + 5):
+        if n < len(items):
+            m, j = items[n]
+            recvs = (fwd_r.at[0, m, j - 1], fwd_r.at[1, m, j - 1])
+            arrived(wout_view(m, j)(part_rows(p)), col_r.at[m, j - 1])
+            if n < passed:
+                mine = wout_view(m, j)(part_rows(p))
+                send(mine, mine, fwd_s.at[0], recvs[0], at(z, xn))
+                send(mine, mine, fwd_s.at[0], recvs[1], at(z, yn))
+            else:
+                share(wout_view(m, j), fwd_s.at[0], *recvs, one_r.at[3])
+        if n >= 5:
+            m, j = items[n - 5]
+            recvs = (fwd_r.at[0, m, j - 1], fwd_r.at[1, m, j - 1])
+            if n - 5 < passed:
+                pass_on(wout_view(m, j), fwd_s.at[0], *recvs, one_r.at[3])
+            else:
+                shared(wout_view(m, j), *recvs)
     finish_block(1, lambda h: ybuf[h].astype(F32))
     arrived(wout.at[pl.ds(0, HL - 1), :, pl.ds(0, part)], one_r.at[3])
 

time: 65.8 us -> 64.9 us (0.986)
  Pallas kernels: 63.1 us -> 62.2 us
    pallas_call x1, Pallas kernels: 63.1 us -> 62.2 us  [one_kernel(): pl.pallas_call(functools.partial(kernel, (cores, HL, G, rows, DH)), out_s...]
where the time goes in v3:
time: 64.9 us; the launch traced here: 64.8 us
  Pallas kernels  62.2 us (96%)
  local copies, waits for them, and re-layouts  1.94 us (3%)
    pallas_call x1, Pallas kernels, one_kernel(): pl.pallas_call(functools.partial(kernel, (cores, HL, G, rows, DH)), out_s...  62.2 us
    unnamed x2, local copies, waits for them, and re-layouts  1.94 us

profile of v3, /device:TPU:0, one launch (start us, length us, event | category | flops | bytes accessed | tf_op | source)
XLA Modules:
  0.0 64.8 jit_solution(14148908173914040641)
XLA Ops:
  0.6 62.2 %shard_map.77 = (bf16[2,128,1024]{2,1,0:T(8,128)(2,1)S(1)}, bf16[4,3,256,256]{3,2,1,0:T(8,128)(2,1)S(1)}) custom-call(bf16[2,128,1024]{2,1,0:T(8,128)(2,1)} %q_hbm.1, bf16[2,128,1024]{2,1,0:T(8,128)(2,1)} %k_hbm.1, bf16[2,128,1024]{2,1,0:T(8,128)(2,1)} %v_hbm.1, f32[2,4,128]{2,1,0:T(4,128)} %r_hbm.1, bf16[4,3,256,256]{3,2,1,0:T(8,128)(2,1)} %w_hbm.1, ...), custom_call_target="tpu_custom_call" | custom-call | tf_op jit(solution)/shard_map/pallas_call | solution.py:394
  62.8 0.8 %copy.10 = bf16[2,128,1024]{2,1,0:T(8,128)(2,1)} copy(bf16[2,128,1024]{2,1,0:T(8,128)(2,1)S(1)} %get-tuple-element.2) | data formatting | bytes 1048576
  63.6 1.1 %copy.11 = bf16[4,3,256,256]{3,2,1,0:T(8,128)(2,1)} copy(bf16[4,3,256,256]{3,2,1,0:T(8,128)(2,1)S(1)} %get-tuple-element.3) | data formatting | bytes 3145728
